TPU v7x, 512 devices: a whole 4x8x8 slice. The times are simulated.
512 devices in a mesh: head: 8 (over y_lo, x), seq: 64 (over y_hi, z, core).
Axes of the slice: x: 4, y: 8 (y_hi: 4, y_lo: 2; y = y_hi * 2 + y_lo), z: 8, core: 2. Of those that a mesh axis runs over, the one named last changes fastest.
Arguments:
- queries: bfloat16 [2, 4096, 4096], P(None, 'seq', 'head'), may hold values from -256 to 256
- keys: bfloat16 [2, 4096, 4096], P(None, 'seq', 'head'), may hold values from -256 to 256
- values: bfloat16 [2, 4096, 4096], P(None, 'seq', 'head'), may hold values from -6 to 6
- token_rates: float32 [1, 16, 4096], P(None, 'head', 'seq'), may hold values from 0.1 to 1
- step_size: float32 [16], P('head'), may hold values from 0.3 to 1
- w_gate: bfloat16 [16, 256, 512], P('head', 'seq'), may hold values from -0.375 to 0.375
- w_up: bfloat16 [16, 256, 512], P('head', 'seq'), may hold values from -0.375 to 0.375
- w_down: bfloat16 [16, 512, 256], P('head', 'seq'), may hold values from -0.25 to 0.25
- norm_gain: float32 [4096], replicated, may hold values from 0.5 to 1.5
Outputs:
- mixed: bfloat16 [2, 4096, 4096], P(None, ('seq', 'head'))
All inputs are finite; a program needn't handle non-finite values.
Results may differ from a plain program's by a relative error of at most 0.0095.
Values may be sent and summed in bfloat16 or wider, within the bound.
No kernel may reach another device: no remote copies, remote signals or barrier semaphores. Data moves between devices by JAX's collectives and lax.ppermute only.
A program may use at most 64 MiB of HBM per device.

v0:
```python
import math
import jax
import jax.numpy as jnp
from jax import lax
from jax.sharding import PartitionSpec as P

DH = 256
DF = 512
WIN = 512
NS_STEPS = 5


def spread(block, axis, holder):
    block = jnp.where(lax.axis_index(axis) == holder, block, jnp.zeros_like(block))
    return lax.psum(block, axis)


def shifted(array, axis, by):
    count = lax.axis_size(axis)
    return lax.ppermute(array, axis, [(i, (i + by) % count) for i in range(count)])


def rms_norm(values_in):
    wide = values_in.astype(jnp.float32)
    mean_square = jnp.mean(wide * wide, axis=-1, keepdims=True)
    return (wide * lax.rsqrt(mean_square + 1e-06)).astype(jnp.bfloat16)


def newton(grad_in):
    norm_value = jnp.sqrt(jnp.sum(grad_in * grad_in))
    iterate = grad_in / (norm_value + 1e-07)
    for _ in range(NS_STEPS):
        gram = jnp.dot(
            iterate, iterate.T, precision=lax.Precision.HIGHEST, preferred_element_type=jnp.float32
        )
        poly = -4.775 * gram + 2.0315 * jnp.dot(
            gram, gram, precision=lax.Precision.HIGHEST, preferred_element_type=jnp.float32
        )
        iterate = 3.4445 * iterate + jnp.dot(
            poly, iterate, precision=lax.Precision.HIGHEST, preferred_element_type=jnp.float32
        )
    return iterate


def orthogonalize(summed, seq_count, seq_index):
    problems = summed.shape[0]
    stride = 1
    problem = jnp.clip(seq_index // stride + 0, 0, problems - 1)
    owned = [newton(lax.dynamic_index_in_dim(summed, problem, 0, keepdims=False))]
    results = []
    for problem_index in range(problems):
        results.append(
            spread(
                owned[problem_index // seq_count].astype(jnp.bfloat16),
                "seq",
                problem_index % seq_count * stride,
            ).astype(jnp.float32)
        )
    return jnp.stack(results)


def body(queries, keys, values, token_rates, step_size, w_gate, w_up, w_down, norm_gain):
    blocks_here, tok_rows, width_here = queries.shape
    head_count = width_here // DH
    seq_count = lax.axis_size("seq")
    seq_index = lax.axis_index("seq")
    gate_fast, up_fast, down_fast = (
        lax.all_gather(w_gate, "seq", axis=1, tiled=True),
        lax.all_gather(w_up, "seq", axis=1, tiled=True),
        lax.all_gather(w_down, "seq", axis=1, tiled=True),
    )
    reach_count = -(-WIN // tok_rows)
    earlier_blocks = []
    for distance in range(1, reach_count + 1):
        arrived = shifted((keys, values), "seq", distance)
        settled = []
        for part_arr in arrived:
            before = jnp.concatenate([jnp.zeros_like(part_arr[:1]), part_arr[:-1]], 0)
            settled.append(jnp.where(seq_index >= distance, part_arr, before))
        earlier_blocks.insert(0, settled)
    context_keys = jnp.concatenate([pair_item[0] for pair_item in earlier_blocks] + [keys], 1)
    context_values = jnp.concatenate([pair_item[1] for pair_item in earlier_blocks] + [values], 1)
    context_len = context_keys.shape[1]
    context_keys = context_keys.reshape(blocks_here, context_len, head_count, DH)
    context_values = context_values.reshape(blocks_here, context_len, head_count, DH)
    query_heads = queries.reshape(blocks_here, tok_rows, head_count, DH)
    key_heads = keys.reshape(blocks_here, tok_rows, head_count, DH)
    value_heads = values.reshape(blocks_here, tok_rows, head_count, DH)
    scores = jnp.einsum(
        "bihd,bjhd->bhij", query_heads, context_keys, preferred_element_type=jnp.float32
    ) * (1.0 / math.sqrt(DH))
    query_rows = jnp.arange(tok_rows, dtype=jnp.int32)
    key_rows = jnp.arange(context_len, dtype=jnp.int32)
    row_gap = reach_count * tok_rows + query_rows[:, None] - key_rows[None, :]
    block_ids = jnp.arange(blocks_here, dtype=jnp.int32)
    key_pos = (
        block_ids[:, None] * (tok_rows * seq_count)
        + seq_index * tok_rows
        - reach_count * tok_rows
        + key_rows[None, :]
    )
    allowed = ((row_gap >= 0) & (row_gap < WIN))[None, :, :] & (key_pos >= 0)[:, None, :]
    scores = jnp.where(allowed[:, None, :, :], scores, -1e30)
    row_top = jnp.max(scores, axis=-1, keepdims=True)
    exp_scores = jnp.exp(scores - row_top)
    attn_weights = (exp_scores / jnp.sum(exp_scores, axis=-1, keepdims=True)).astype(jnp.bfloat16)
    attention = jnp.einsum(
        "bhij,bjhd->bihd", attn_weights, context_values, preferred_element_type=jnp.float32
    )
    query_norm = rms_norm(query_heads)
    key_norm = rms_norm(key_heads[: blocks_here - 1])
    fast_parts = []
    for block_index in range(blocks_here):
        gate_query = jnp.einsum(
            "thd,hdf->htf", query_norm[block_index], gate_fast, preferred_element_type=jnp.float32
        )
        up_query = jnp.einsum(
            "thd,hdf->htf", query_norm[block_index], up_fast, preferred_element_type=jnp.float32
        )
        hidden = (jax.nn.silu(gate_query) * up_query).astype(jnp.bfloat16)
        fast_parts.append(
            jnp.einsum("htf,hfd->thd", hidden, down_fast, preferred_element_type=jnp.float32)
        )
        if block_index < blocks_here - 1:
            keys_now = key_norm[block_index]
            vals_now = value_heads[block_index]
            gate_pre = jnp.einsum(
                "thd,hdf->htf", keys_now, gate_fast, preferred_element_type=jnp.float32
            )
            up_pre = jnp.einsum(
                "thd,hdf->htf", keys_now, up_fast, preferred_element_type=jnp.float32
            )
            back = jnp.einsum(
                "thd,hfd->htf", vals_now, down_fast, preferred_element_type=jnp.float32
            )
            rate_col = token_rates[block_index][:, :, None]
            sigmoid_val = jax.nn.sigmoid(gate_pre)
            act_val = gate_pre * sigmoid_val
            d_gate = (
                rate_col * back * up_pre * sigmoid_val * (1.0 + gate_pre * (1.0 - sigmoid_val))
            ).astype(jnp.bfloat16)
            d_up = (rate_col * back * act_val).astype(jnp.bfloat16)
            h_rate = (rate_col * act_val * up_pre).astype(jnp.bfloat16)
            grad_gate = jnp.einsum(
                "thd,htf->hdf", keys_now, d_gate, preferred_element_type=jnp.float32
            )
            grad_up = jnp.einsum("thd,htf->hdf", keys_now, d_up, preferred_element_type=jnp.float32)
            grad_down_t = jnp.einsum(
                "thd,htf->hdf", vals_now, h_rate, preferred_element_type=jnp.float32
            )
            stacked = jnp.stack([grad_gate, grad_up, grad_down_t], 1).reshape(
                head_count * 3, DH, DF
            )
            summed = lax.psum(stacked, "seq")
            orthogonal = orthogonalize(summed, seq_count, seq_index).reshape(head_count, 3, DH, DF)
            step_col = step_size[:, None, None]
            gate_fast = (gate_fast.astype(jnp.float32) + step_col * orthogonal[:, 0]).astype(
                jnp.bfloat16
            )
            up_fast = (up_fast.astype(jnp.float32) + step_col * orthogonal[:, 1]).astype(
                jnp.bfloat16
            )
            down_fast = (
                down_fast.astype(jnp.float32) + step_col * jnp.swapaxes(orthogonal[:, 2], 1, 2)
            ).astype(jnp.bfloat16)
    fast_out = jnp.stack(fast_parts)
    combined = (
        (fast_out + attention).astype(jnp.bfloat16).reshape(blocks_here, tok_rows, width_here)
    )
    wide = lax.all_to_all(combined, "head", split_axis=1, concat_axis=2, tiled=True).astype(
        jnp.float32
    )
    mean_square = jnp.mean(wide * wide, axis=-1, keepdims=True)
    return (wide * lax.rsqrt(mean_square + 1e-06) * norm_gain).astype(jnp.bfloat16)


def solution(mesh):
    placed = (
        P(None, "seq", "head"),
        P(None, "seq", "head"),
        P(None, "seq", "head"),
        P(None, "head", "seq"),
        P("head"),
        P("head", "seq", None),
        P("head", "seq", None),
        P("head", "seq", None),
        P(),
    )
    return jax.shard_map(
        body, mesh=mesh, in_specs=placed, out_specs=P(None, ("seq", "head"), None), check_vma=False
    )
```

profile of v0, /device:TPU:1, one launch (start us, length us, event | category | flops | bytes accessed | tf_op | source)
XLA Modules:
  0.0 1475.3 jit_solution(10621219490444785268)
XLA Ops:
  6.5 11.6 collective-permute-start
  18.1 2.5 collective-permute-start.1
  20.6 6.6 collective-permute-start.2
  27.2 5.8 collective-permute-start.3
  33.0 4.0 collective-permute-start.4
  37.1 0.9 fusion.87
  37.9 0.9 slice_convert_fusion
  38.8 0.8 slice.75
  40.1 88.6 %all_gather.9 = bf16[2,256,512]{2,0,1:T(2,128)(2,1)S(1)} all-gather(bf16[2,4,512]{2,0,1:T(2,128)(2,1)S(1)} %copy.91), channel_id=1, replica_groups=mesh['head'=8,'seq'=64] {'seq'}, dimensions={1}, use_global_device_ids=true | all-gather | bytes 532480 | tf_op jit(solution)/shard_map/all_gather | solution.py:68
  128.6 80.5 %all_gather.10 = bf16[2,256,512]{2,0,1:T(2,128)(2,1)S(1)} all-gather(bf16[2,4,512]{2,0,1:T(2,128)(2,1)S(1)} %copy.93), channel_id=1, replica_groups=mesh['head'=8,'seq'=64] {'seq'}, dimensions={1}, use_global_device_ids=true | all-gather | bytes 532480 | tf_op jit(solution)/shard_map/all_gather | solution.py:69
  209.7 77.9 %all_gather.11 = bf16[2,512,256]{2,0,1:T(2,128)(2,1)S(1)} all-gather(bf16[2,8,256]{2,0,1:T(2,128)(2,1)S(1)} %copy.95), channel_id=1, replica_groups=mesh['head'=8,'seq'=64] {'seq'}, dimensions={1}, use_global_device_ids=true | all-gather | bytes 532480 | tf_op jit(solution)/shard_map/all_gather | solution.py:70
  290.2 2.0 copy.106
  293.3 0.9 fusion.57
  294.4 1.9 collective-permute-start.5
  296.5 3.4 collective-permute-start.6
  299.9 1.9 collective-permute-start.8
  301.9 1.9 collective-permute-start.9
  303.8 4.7 collective-permute-start.10
  308.5 11.1 collective-permute-start.11
  319.7 3.0 collective-permute-start.12
  322.8 2.7 collective-permute-start.13
  325.5 3.4 collective-permute-done.9
  328.9 1.9 collective-permute-start.14
  330.8 5.3 collective-permute-done.10
  336.1 1.9 collective-permute-start.15
  338.0 2.3 collective-permute-done.11
  340.3 5.9 collective-permute-start.7
  346.3 2.0 convolution_bitcast_fusion.4
  348.4 1.0 slice.102
  349.5 0.9 slice.105
  351.2 9.3 collective-permute-done.14
  360.5 0.9 slice.108
  366.0 1.0 copy-done.34
  367.7 503.6 %all-reduce.20.cloned.1.call-done = f32[6,256,512]{2,1,0:T(8,128)} async-done(((f32[6,256,512]{2,1,0:T(8,128)}), f32[6,256,512]{2,1,0:T(8,128)}) %all-reduce.20.cloned.1.call-update) | async-done | bytes 3145744 | tf_op jit(solution)/shard_map/psum | solution.py:154
  871.3 1.8 multiply_reduce_fusion
  873.8 1.8 fusion.43
  876.0 1.9 convolution_add_fusion.4
  883.9 1.9 select_bitcast_fusion
  885.8 0.8 copy-done.18
  888.7 1.7 select_dynamic-update-slice_fusion
  891.8 1.7 fusion.4
  893.8 555.3 %all-reduce.22.cloned.1.call-done = (bf16[1,256,512]{2,1,0:T(8,128)(2,1)}, bf16[1,256,512]{2,1,0:T(8,128)(2,1)}, bf16[1,256,512]{2,1,0:T(8,128)(2,1)}, bf16[1,25...) async-done(((bf16[1,256,512]{2,1,0:T(8,128)(2,1)}, bf16[1,256,512]{2,1,0:T(8,128)(2,1)}, bf16[1,256,512]{2,1,0:T(8,128)(2,1)}, ...) | async-done | bytes 1572880 | tf_op jit(solution)/shard_map/psum | solution.py:15
  1449.1 1.0 constant_dynamic-update-slice_fusion.5
  1450.2 1.0 constant_dynamic-update-slice_fusion.4
  1451.8 1.7 copy-done
  1453.8 2.1 convolution_bitcast_fusion.3
  1455.9 1.8 fusion.24
  1457.9 9.3 all_to_all.4
  (190 shorter events, 23.2 us)
Async XLA Ops:
  6.5 33.5 %copy-start.35 = (bf16[2,4,512]{2,1,0:T(4,128)(2,1)S(1)}, bf16[2,4,512]{2,1,0:T(4,128)(2,1)}, u32[]{:S(2)}) copy-start(bf16[2,4,512]{2,1,0:T(4,128)(2,1)} %param.14) | copy-start | bytes 24580
  6.5 122.1 %copy-start.36 = (bf16[2,4,512]{2,1,0:T(4,128)(2,1)S(1)}, bf16[2,4,512]{2,1,0:T(4,128)(2,1)}, u32[]{:S(2)}) copy-start(bf16[2,4,512]{2,1,0:T(4,128)(2,1)} %param.15) | copy-start | bytes 24580
  6.5 864.8 %all-reduce.20.cloned.1.call-start = ((), (), s32[]{:S(2)}) async-start(), calls=%async_computation.1 | async-start | bytes 6291456 | tf_op jit(solution)/shard_map/psum | solution.py:154
  6.5 287.9 %collective-permute-start = (bf16[2,64,512]{2,1,0:T(8,128)(2,1)}, bf16[2,64,512]{2,1,0:T(8,128)(2,1)S(1)}, u32[]{:S(2)}, u32[]{:S(2)}) collective-permute-start(bf16[2,64,512]{2,1,0:T(8,128)(2,1)} %param.11), channel_id=1, source_target_pairs={{0,8},{1,9},{2,10},{3,11},{4,12},{5,13},{6,14},{7,15},{8,16},{9,17... | collective-permute-start | bytes 393224 | tf_op jit(solution)/shard_map/ppermute | solution.py:20
  18.1 278.3 %collective-permute-start.1 = (bf16[2,64,512]{2,1,0:T(8,128)(2,1)}, bf16[2,64,512]{2,1,0:T(8,128)(2,1)S(1)}, u32[]{:S(2)}, u32[]{:S(2)}) collective-permute-start(bf16[2,64,512]{2,1,0:T(8,128)(2,1)} %param.11), channel_id=1, source_target_pairs={{0,7},{1,8},{2,9},{3,10},{4,11},{5,12},{6,13},{7,14},{8,15},{9,16}... | collective-permute-start | bytes 393224 | tf_op jit(solution)/shard_map/ppermute | solution.py:20
  20.6 279.3 %collective-permute-start.2 = (bf16[2,64,512]{2,1,0:T(8,128)(2,1)}, bf16[2,64,512]{2,1,0:T(8,128)(2,1)S(1)}, u32[]{:S(2)}, u32[]{:S(2)}) collective-permute-start(bf16[2,64,512]{2,1,0:T(8,128)(2,1)} %param.11), channel_id=1, source_target_pairs={{0,6},{1,7},{2,8},{3,9},{4,10},{5,11},{6,12},{7,13},{8,14},{9,15},... | collective-permute-start | bytes 393224 | tf_op jit(solution)/shard_map/ppermute | solution.py:20
  27.2 274.7 %collective-permute-start.3 = (bf16[2,64,512]{2,1,0:T(8,128)(2,1)}, bf16[2,64,512]{2,1,0:T(8,128)(2,1)S(1)}, u32[]{:S(2)}, u32[]{:S(2)}) collective-permute-start(bf16[2,64,512]{2,1,0:T(8,128)(2,1)} %param.11), channel_id=1, source_target_pairs={{0,5},{1,6},{2,7},{3,8},{4,9},{5,10},{6,11},{7,12},{8,13},{9,14},{... | collective-permute-start | bytes 393224 | tf_op jit(solution)/shard_map/ppermute | solution.py:20
  33.0 270.8 %collective-permute-start.4 = (bf16[2,64,512]{2,1,0:T(8,128)(2,1)}, bf16[2,64,512]{2,1,0:T(8,128)(2,1)S(1)}, u32[]{:S(2)}, u32[]{:S(2)}) collective-permute-start(bf16[2,64,512]{2,1,0:T(8,128)(2,1)} %param.11), channel_id=1, source_target_pairs={{0,4},{1,5},{2,6},{3,7},{4,8},{5,9},{6,10},{7,11},{8,12},{9,13},{1... | collective-permute-start | bytes 393224 | tf_op jit(solution)/shard_map/ppermute | solution.py:20
  128.6 81.0 %copy-start.37 = (bf16[2,8,256]{2,1,0:T(8,128)(2,1)S(1)}, bf16[2,8,256]{2,1,0:T(8,128)(2,1)}, u32[]{:S(2)}) copy-start(bf16[2,8,256]{2,1,0:T(8,128)(2,1)} %param.16) | copy-start | bytes 24580
  209.4 78.9 %copy-start.38 = (f32[1,2,64]{2,1,0:T(2,128)S(1)}, f32[1,2,64]{2,1,0:T(2,128)}, u32[]{:S(2)}) copy-start(f32[1,2,64]{2,1,0:T(2,128)} %param.12) | copy-start | bytes 1540
  292.2 7.7 copy-start.1
  292.2 1156.9 %all-reduce.22.cloned.1.call-start = ((), (), s32[]{:S(2)}) async-start(), calls=%async_computation.2 | async-start | bytes 3145728 | tf_op jit(solution)/shard_map/psum | solution.py:15
  294.4 53.9 %copy-start.11 = (bf16[2,64,512]{2,1,0:T(8,128)(2,1)}, bf16[2,64,512]{2,1,0:T(8,128)(2,1)S(1)}, u32[]{:S(2)}) copy-start(bf16[2,64,512]{2,1,0:T(8,128)(2,1)S(1)} %collective-permute-done) | copy-start | bytes 393220
  294.4 14.1 collective-permute-start.5
  296.4 51.9 %copy-start.9 = (bf16[2,64,512]{2,1,0:T(8,128)(2,1)}, bf16[2,64,512]{2,1,0:T(8,128)(2,1)S(1)}, u32[]{:S(2)}) copy-start(bf16[2,64,512]{2,1,0:T(8,128)(2,1)S(1)} %collective-permute-done.1) | copy-start | bytes 393220
  296.5 23.2 %collective-permute-start.6 = (bf16[2,64,512]{2,1,0:T(8,128)(2,1)S(1)}, bf16[2,64,512]{2,1,0:T(8,128)(2,1)S(1)}, u32[]{:S(2)}, u32[]{:S(2)}) collective-permute-start(bf16[2,64,512]{2,1,0:T(8,128)(2,1)S(1)} %copy-done.27), channel_id=1, source_target_pairs={{0,2},{1,3},{2,4},{3,5},{4,6},{5,7},{6,8},{7,9},{8,10},{9,11},{10,... | collective-permute-start | bytes 393224 | tf_op jit(solution)/shard_map/ppermute | solution.py:20
  299.9 48.4 %copy-start.7 = (bf16[2,64,512]{2,1,0:T(8,128)(2,1)}, bf16[2,64,512]{2,1,0:T(8,128)(2,1)S(1)}, u32[]{:S(2)}) copy-start(bf16[2,64,512]{2,1,0:T(8,128)(2,1)S(1)} %collective-permute-done.2) | copy-start | bytes 393220
  299.9 22.8 %collective-permute-start.8 = (bf16[2,64,512]{2,1,0:T(8,128)(2,1)S(1)}, bf16[2,64,512]{2,1,0:T(8,128)(2,1)S(1)}, u32[]{:S(2)}, u32[]{:S(2)}) collective-permute-start(bf16[2,64,512]{2,1,0:T(8,128)(2,1)S(1)} %copy-done.1), channel_id=1, source_target_pairs={{0,8},{1,9},{2,10},{3,11},{4,12},{5,13},{6,14},{7,15},{8,16},{9,17... | collective-permute-start | bytes 393224 | tf_op jit(solution)/shard_map/ppermute | solution.py:20
  301.9 46.5 %copy-start.5 = (bf16[2,64,512]{2,1,0:T(8,128)(2,1)}, bf16[2,64,512]{2,1,0:T(8,128)(2,1)S(1)}, u32[]{:S(2)}) copy-start(bf16[2,64,512]{2,1,0:T(8,128)(2,1)S(1)} %collective-permute-done.3) | copy-start | bytes 393220
  301.9 27.0 %collective-permute-start.9 = (bf16[2,64,512]{2,1,0:T(8,128)(2,1)S(1)}, bf16[2,64,512]{2,1,0:T(8,128)(2,1)}, u32[]{:S(2)}, u32[]{:S(2)}) collective-permute-start(bf16[2,64,512]{2,1,0:T(8,128)(2,1)S(1)} %copy-done.1), channel_id=1, source_target_pairs={{0,7},{1,8},{2,9},{3,10},{4,11},{5,12},{6,13},{7,14},{8,15},{9,16}... | collective-permute-start | bytes 393224 | tf_op jit(solution)/shard_map/ppermute | solution.py:20
  303.8 44.6 %copy-start.3 = (bf16[2,64,512]{2,1,0:T(8,128)(2,1)}, bf16[2,64,512]{2,1,0:T(8,128)(2,1)S(1)}, u32[]{:S(2)}) copy-start(bf16[2,64,512]{2,1,0:T(8,128)(2,1)S(1)} %collective-permute-done.4) | copy-start | bytes 393220
  303.8 32.2 %collective-permute-start.10 = (bf16[2,64,512]{2,1,0:T(8,128)(2,1)S(1)}, bf16[2,64,512]{2,1,0:T(8,128)(2,1)S(1)}, u32[]{:S(2)}, u32[]{:S(2)}) collective-permute-start(bf16[2,64,512]{2,1,0:T(8,128)(2,1)S(1)} %copy-done.1), channel_id=1, source_target_pairs={{0,6},{1,7},{2,8},{3,9},{4,10},{5,11},{6,12},{7,13},{8,14},{9,15},... | collective-permute-start | bytes 393224 | tf_op jit(solution)/shard_map/ppermute | solution.py:20
  308.5 39.9 %copy-start.19 = (bf16[2,64,512]{2,1,0:T(8,128)(2,1)}, bf16[2,64,512]{2,1,0:T(8,128)(2,1)S(1)}, u32[]{:S(2)}) copy-start(bf16[2,64,512]{2,1,0:T(8,128)(2,1)S(1)} %collective-permute-done.5) | copy-start | bytes 393220
  308.5 31.8 %collective-permute-start.11 = (bf16[2,64,512]{2,1,0:T(8,128)(2,1)S(1)}, bf16[2,64,512]{2,1,0:T(8,128)(2,1)S(1)}, u32[]{:S(2)}, u32[]{:S(2)}) collective-permute-start(bf16[2,64,512]{2,1,0:T(8,128)(2,1)S(1)} %copy-done.1), channel_id=1, source_target_pairs={{0,5},{1,6},{2,7},{3,8},{4,9},{5,10},{6,11},{7,12},{8,13},{9,14},{... | collective-permute-start | bytes 393224 | tf_op jit(solution)/shard_map/ppermute | solution.py:20
  319.7 28.7 %copy-start.13 = (bf16[2,64,512]{2,1,0:T(8,128)(2,1)}, bf16[2,64,512]{2,1,0:T(8,128)(2,1)S(1)}, u32[]{:S(2)}) copy-start(bf16[2,64,512]{2,1,0:T(8,128)(2,1)S(1)} %collective-permute-done.6) | copy-start | bytes 393220
  319.7 29.7 %collective-permute-start.12 = (bf16[2,64,512]{2,1,0:T(8,128)(2,1)S(1)}, bf16[2,64,512]{2,1,0:T(8,128)(2,1)}, u32[]{:S(2)}, u32[]{:S(2)}) collective-permute-start(bf16[2,64,512]{2,1,0:T(8,128)(2,1)S(1)} %copy-done.1), channel_id=1, source_target_pairs={{0,4},{1,5},{2,6},{3,7},{4,8},{5,9},{6,10},{7,11},{8,12},{9,13},{1... | collective-permute-start | bytes 393224 | tf_op jit(solution)/shard_map/ppermute | solution.py:20
  322.8 28.4 %collective-permute-start.13 = (bf16[2,64,512]{2,1,0:T(8,128)(2,1)S(1)}, bf16[2,64,512]{2,1,0:T(8,128)(2,1)S(1)}, u32[]{:S(2)}, u32[]{:S(2)}) collective-permute-start(bf16[2,64,512]{2,1,0:T(8,128)(2,1)S(1)} %copy-done.1), channel_id=1, source_target_pairs={{0,3},{1,4},{2,5},{3,6},{4,7},{5,8},{6,9},{7,10},{8,11},{9,12},{10... | collective-permute-start | bytes 393224 | tf_op jit(solution)/shard_map/ppermute | solution.py:20
  328.9 31.6 %collective-permute-start.14 = (bf16[2,64,512]{2,1,0:T(8,128)(2,1)S(1)}, bf16[2,64,512]{2,1,0:T(8,128)(2,1)S(1)}, u32[]{:S(2)}, u32[]{:S(2)}) collective-permute-start(bf16[2,64,512]{2,1,0:T(8,128)(2,1)S(1)} %copy-done.1), channel_id=1, source_target_pairs={{0,2},{1,3},{2,4},{3,5},{4,6},{5,7},{6,8},{7,9},{8,10},{9,11},{10,... | collective-permute-start | bytes 393224 | tf_op jit(solution)/shard_map/ppermute | solution.py:20
  336.1 12.2 copy-start.23
  336.1 24.4 %collective-permute-start.15 = (bf16[2,64,512]{2,1,0:T(8,128)(2,1)S(1)}, bf16[2,64,512]{2,1,0:T(8,128)(2,1)}, u32[]{:S(2)}, u32[]{:S(2)}) collective-permute-start(bf16[2,64,512]{2,1,0:T(8,128)(2,1)S(1)} %copy-done.1), channel_id=1, source_target_pairs={{0,1},{1,2},{2,3},{3,4},{4,5},{5,6},{6,7},{7,8},{8,9},{9,10},{10,1... | collective-permute-start | bytes 393224 | tf_op jit(solution)/shard_map/ppermute | solution.py:20
  340.3 8.0 copy-start.21
  340.3 21.1 %collective-permute-start.7 = (bf16[2,64,512]{2,1,0:T(8,128)(2,1)}, bf16[2,64,512]{2,1,0:T(8,128)(2,1)}, u32[]{:S(2)}, u32[]{:S(2)}) collective-permute-start(bf16[2,64,512]{2,1,0:T(8,128)(2,1)} %param.11), channel_id=1, source_target_pairs={{0,1},{1,2},{2,3},{3,4},{4,5},{5,6},{6,7},{7,8},{8,9},{9,10},{10,1... | collective-permute-start | bytes 393224 | tf_op jit(solution)/shard_map/ppermute | solution.py:20
  348.3 13.9 copy-start.12
  348.3 13.9 slice-start.4
  348.3 14.6 copy-start.26
  348.3 14.6 slice-start.11
  348.4 14.6 copy-start.10
  348.4 14.6 slice-start.3
  348.4 15.3 %copy-start.8 = (bf16[2,64,512]{2,1,0:T(8,128)(2,1)S(1)}, bf16[2,64,512]{2,1,0:T(8,128)(2,1)}, u32[]{:S(2)}) copy-start(bf16[2,64,512]{2,1,0:T(8,128)(2,1)} %copy-done.7) | copy-start | bytes 393220
  348.4 15.3 %slice-start.2 = ((bf16[2,64,512]{2,1,0:T(8,128)(2,1)}), bf16[1,64,512]{2,1,0:T(8,128)(2,1)S(1)}, s32[]{:S(2)}) async-start(bf16[2,64,512]{2,1,0:T(8,128)(2,1)} %copy-done.7), calls=%async_computation.5 | async-start | bytes 131072 | tf_op jit(solution)/shard_map/slice | solution.py:78
  349.4 15.0 %copy-start.24 = (bf16[2,64,512]{2,1,0:T(8,128)(2,1)S(1)}, bf16[2,64,512]{2,1,0:T(8,128)(2,1)}, u32[]{:S(2)}) copy-start(bf16[2,64,512]{2,1,0:T(8,128)(2,1)} %copy-done.23) | copy-start | bytes 393220
  349.4 15.0 %slice-start.10 = ((bf16[2,64,512]{2,1,0:T(8,128)(2,1)}), bf16[1,64,512]{2,1,0:T(8,128)(2,1)S(1)}, s32[]{:S(2)}) async-start(bf16[2,64,512]{2,1,0:T(8,128)(2,1)} %copy-done.23), calls=%async_computation.13 | async-start | bytes 131072 | tf_op jit(solution)/shard_map/slice | solution.py:78
  351.2 13.4 copy-start.17
  351.2 13.4 copy-start.6
  351.2 13.4 slice-start.1
  360.5 4.0 copy-start.15
  886.7 4.5 copy-start.28
  1457.6 10.1 copy-start.33
  (23 other events, 46.9 us)
Sparse Core Ops, SparseCore 0:
  292.3 578.9 all-reduce.19
  885.9 563.1 all-reduce.21
where the time goes:
time: 1480 us
  waiting for transfers between devices  1080 us (73%)
  blocking collectives  256 us (17%)
  starting transfers between devices  71 us (5%)
  matrix products  22.4 us (2%)
  local copies, waits for them, and re-layouts  15.9 us (1%)
  between operations  15.2 us (1%)
    psum x1, waiting for transfers between devices, spread(): return lax.psum(block, axis)  555 us
    psum x1, waiting for transfers between devices, body(): summed = lax.psum(stacked, 'seq')  504 us
    all_gather x1, blocking collectives, body(): lax.all_gather(w_gate, 'seq', axis=1, tiled=True)  88.6 us
    all_gather x1, blocking collectives, body(): lax.all_gather(w_up, 'seq', axis=1, tiled=True)  80.5 us
    all_gather x1, blocking collectives, body(): lax.all_gather(w_down, 'seq', axis=1, tiled=True)  77.9 us
    ppermute x16, starting transfers between devices, shifted(): lax.ppermute(array, axis, [(i, (i + by) % count) for i in range(count)])  70.9 us
  transfers between devices with their start and end apart: 18, of which 7 were waited for; matrix products, arithmetic and copies ran while one was open for 2% of the time, Pallas kernels for 0%

commit v1 on v0

--- a/solution.py
+++ b/solution.py
@@ -67,7 +67,9 @@
     gate_fast, up_fast, down_fast = (
         lax.all_gather(w_gate, "seq", axis=1, tiled=True),
         lax.all_gather(w_up, "seq", axis=1, tiled=True),
-        lax.all_gather(w_down, "seq", axis=1, tiled=True),
+        jnp.concatenate(
+            lax.all_to_all(jnp.stack([w_down] * lax.axis_size("seq")), "seq", 0, 0), axis=1
+        ),
     )
     reach_count = -(-WIN // tok_rows)
     earlier_blocks = []

time: 1480 us -> 1420 us (0.959)
  blocking collectives: 256 us -> 183 us
    all_gather x1 -> x0, blocking collectives: 77.9 us -> none  [body(): lax.all_gather(w_down, 'seq', axis=1, tiled=True)]
    psum x1, waiting for transfers between devices: 504 us -> 523 us  [body(): summed = lax.psum(stacked, 'seq')]
  transfers between devices with their start and end apart: 18 -> 19, of which waited for: 7 -> 7; matrix products, arithmetic and copies ran while one was open for 2% -> 3% of each run, Pallas kernels for 0% -> 0%
where the time goes in v1:
time: 1420 us
  waiting for transfers between devices  1090 us (77%)
  blocking collectives  183 us (13%)
  starting transfers between devices  74.8 us (5%)
  local copies, waits for them, and re-layouts  25.1 us (2%)
  matrix products  21.6 us (2%)
  between operations  14.9 us (1%)
    psum x1, waiting for transfers between devices, spread(): return lax.psum(block, axis)  555 us
    psum x1, waiting for transfers between devices, body(): summed = lax.psum(stacked, 'seq')  523 us
    all_gather x1, blocking collectives, body(): lax.all_gather(w_gate, 'seq', axis=1, tiled=True)  95.8 us
    all_gather x1, blocking collectives, body(): lax.all_gather(w_up, 'seq', axis=1, tiled=True)  77.9 us
    ppermute x16, starting transfers between devices, shifted(): lax.ppermute(array, axis, [(i, (i + by) % count) for i in range(count)])  66.6 us
  transfers between devices with their start and end apart: 19, of which 7 were waited for; matrix products, arithmetic and copies ran while one was open for 3% of the time, Pallas kernels for 0%

profile of v1, /device:TPU:1, one launch (start us, length us, event | category | flops | bytes accessed | tf_op | source)
XLA Modules:
  0.0 1420.5 jit_solution(10936810479203637554)
XLA Ops:
  6.5 11.6 collective-permute-start
  18.1 2.5 collective-permute-start.1
  20.6 6.6 collective-permute-start.2
  27.2 5.8 collective-permute-start.3
  33.0 4.0 collective-permute-start.4
  37.1 1.5 stack.37
  38.6 8.1 all-to-all-start
  47.3 95.8 %all_gather.6 = bf16[2,256,512]{2,0,1:T(2,128)(2,1)S(1)} all-gather(bf16[2,4,512]{2,0,1:T(2,128)(2,1)S(1)} %copy.87), channel_id=1, replica_groups=mesh['head'=8,'seq'=64] {'seq'}, dimensions={1}, use_global_device_ids=true | all-gather | bytes 532480 | tf_op jit(solution)/shard_map/all_gather | solution.py:68
  143.7 77.9 %all_gather.7 = bf16[2,256,512]{2,0,1:T(2,128)(2,1)S(1)} all-gather(bf16[2,4,512]{2,0,1:T(2,128)(2,1)S(1)} %copy.89), channel_id=1, replica_groups=mesh['head'=8,'seq'=64] {'seq'}, dimensions={1}, use_global_device_ids=true | all-gather | bytes 532480 | tf_op jit(solution)/shard_map/all_gather | solution.py:69
  223.6 1.0 fusion.51
  224.6 1.0 fusion.73
  227.1 2.0 copy.99
  230.0 1.9 collective-permute-start.5
  231.9 1.9 collective-permute-start.8
  233.9 1.9 collective-permute-start.9
  235.9 3.4 collective-permute-start.10
  239.3 9.6 collective-permute-start.11
  248.9 7.3 collective-permute-start.12
  256.2 2.2 collective-permute-start.13
  259.1 0.8 slice.109
  261.7 0.8 slice.112
  262.5 0.8 slice.113
  263.4 1.2 collective-permute-done.9
  264.6 1.9 collective-permute-start.6
  266.5 4.1 collective-permute-done.10
  270.6 1.9 collective-permute-start.14
  272.5 3.6 collective-permute-done.11
  276.1 1.9 collective-permute-start.15
  278.6 2.1 collective-permute-start.7
  280.7 0.9 collective-permute-done.13
  285.3 1.0 copy-done.17
  287.0 523.0 %all-reduce.20.cloned.1.call-done = f32[6,256,512]{2,1,0:T(8,128)} async-done(((f32[6,256,512]{2,1,0:T(8,128)}), f32[6,256,512]{2,1,0:T(8,128)}) %all-reduce.20.cloned.1.call-update) | async-done | bytes 3145744 | tf_op jit(solution)/shard_map/psum | solution.py:156
  810.0 1.8 multiply_reduce_fusion
  812.4 1.8 fusion.38
  814.6 1.9 convolution_add_fusion.4
  822.5 1.9 select_bitcast_fusion
  824.4 0.9 copy-done.5
  829.5 1.8 fusion.4
  832.9 554.7 %all-reduce.22.cloned.1.call-done = (bf16[1,256,512]{2,1,0:T(8,128)(2,1)}, bf16[1,256,512]{2,1,0:T(8,128)(2,1)}, bf16[1,256,512]{2,1,0:T(8,128)(2,1)}, bf16[1,25...) async-done(((bf16[1,256,512]{2,1,0:T(8,128)(2,1)}, bf16[1,256,512]{2,1,0:T(8,128)(2,1)}, bf16[1,256,512]{2,1,0:T(8,128)(2,1)}, ...) | async-done | bytes 1572880 | tf_op jit(solution)/shard_map/psum | solution.py:15
  1387.5 1.0 constant_dynamic-update-slice_fusion.5
  1388.6 1.0 constant_dynamic-update-slice_fusion.4
  1389.8 1.8 fusion.87
  1391.5 1.6 copy.121
  1393.1 2.6 copy.122
  1395.7 2.5 copy.123
  1398.5 2.1 convolution_bitcast_fusion.3
  1400.6 2.2 fusion.24
  1403.1 9.4 all_to_all.14
  (147 shorter events, 26.5 us)
Async XLA Ops:
  6.5 40.3 %copy-start.1 = (bf16[2,64,512]{2,1,0:T(8,128)(2,1)S(1)}, bf16[2,64,512]{2,1,0:T(8,128)(2,1)}, u32[]{:S(2)}) copy-start(bf16[2,64,512]{2,1,0:T(8,128)(2,1)} %param.10) | copy-start | bytes 393220
  6.5 222.8 %collective-permute-start = (bf16[2,64,512]{2,1,0:T(8,128)(2,1)}, bf16[2,64,512]{2,1,0:T(8,128)(2,1)}, u32[]{:S(2)}, u32[]{:S(2)}) collective-permute-start(bf16[2,64,512]{2,1,0:T(8,128)(2,1)} %param.11), channel_id=1, source_target_pairs={{0,8},{1,9},{2,10},{3,11},{4,12},{5,13},{6,14},{7,15},{8,16},{9,17... | collective-permute-start | bytes 393224 | tf_op jit(solution)/shard_map/ppermute | solution.py:20
  18.1 213.8 %collective-permute-start.1 = (bf16[2,64,512]{2,1,0:T(8,128)(2,1)}, bf16[2,64,512]{2,1,0:T(8,128)(2,1)}, u32[]{:S(2)}, u32[]{:S(2)}) collective-permute-start(bf16[2,64,512]{2,1,0:T(8,128)(2,1)} %param.11), channel_id=1, source_target_pairs={{0,7},{1,8},{2,9},{3,10},{4,11},{5,12},{6,13},{7,14},{8,15},{9,16}... | collective-permute-start | bytes 393224 | tf_op jit(solution)/shard_map/ppermute | solution.py:20
  20.6 213.3 %collective-permute-start.2 = (bf16[2,64,512]{2,1,0:T(8,128)(2,1)}, bf16[2,64,512]{2,1,0:T(8,128)(2,1)}, u32[]{:S(2)}, u32[]{:S(2)}) collective-permute-start(bf16[2,64,512]{2,1,0:T(8,128)(2,1)} %param.11), channel_id=1, source_target_pairs={{0,6},{1,7},{2,8},{3,9},{4,10},{5,11},{6,12},{7,13},{8,14},{9,15},... | collective-permute-start | bytes 393224 | tf_op jit(solution)/shard_map/ppermute | solution.py:20
  27.2 208.7 %collective-permute-start.3 = (bf16[2,64,512]{2,1,0:T(8,128)(2,1)}, bf16[2,64,512]{2,1,0:T(8,128)(2,1)}, u32[]{:S(2)}, u32[]{:S(2)}) collective-permute-start(bf16[2,64,512]{2,1,0:T(8,128)(2,1)} %param.11), channel_id=1, source_target_pairs={{0,5},{1,6},{2,7},{3,8},{4,9},{5,10},{6,11},{7,12},{8,13},{9,14},{... | collective-permute-start | bytes 393224 | tf_op jit(solution)/shard_map/ppermute | solution.py:20
  33.0 206.2 %collective-permute-start.4 = (bf16[2,64,512]{2,1,0:T(8,128)(2,1)}, bf16[2,64,512]{2,1,0:T(8,128)(2,1)}, u32[]{:S(2)}, u32[]{:S(2)}) collective-permute-start(bf16[2,64,512]{2,1,0:T(8,128)(2,1)} %param.11), channel_id=1, source_target_pairs={{0,4},{1,5},{2,6},{3,7},{4,8},{5,9},{6,10},{7,11},{8,12},{9,13},{1... | collective-permute-start | bytes 393224 | tf_op jit(solution)/shard_map/ppermute | solution.py:20
  38.6 8.7 copy-start.18
  38.6 187.1 %all-to-all-start = ((bf16[64,2,8,256]{3,2,1,0:T(8,128)(2,1)}), bf16[64,2,8,256]{3,2,1,0:T(8,128)(2,1)S(1)}, u32[]{:S(2)}, u32[]{:S(2)}) async-start(bf16[64,2,8,256]{3,2,1,0:T(8,128)(2,1)} %stack.37), calls=%async_computation | async-start | bytes 1048576 | tf_op jit(solution)/shard_map/all_to_all | solution.py:71
  46.7 763.2 %all-reduce.20.cloned.1.call-start = ((), (), s32[]{:S(2)}) async-start(), calls=%async_computation.2 | async-start | bytes 6291456 | tf_op jit(solution)/shard_map/psum | solution.py:156
  46.8 96.8 %copy-start.19 = (bf16[2,4,512]{2,1,0:T(4,128)(2,1)S(1)}, bf16[2,4,512]{2,1,0:T(4,128)(2,1)}, u32[]{:S(2)}) copy-start(bf16[2,4,512]{2,1,0:T(4,128)(2,1)} %param.15) | copy-start | bytes 24580
  222.2 0.9 copy-start.8
  222.2 1.0 copy-start.2
  222.2 1.1 copy-start.21
  229.1 0.9 copy-start.9
  229.1 1158.4 %all-reduce.22.cloned.1.call-start = ((), (), s32[]{:S(2)}) async-start(), calls=%async_computation.3 | async-start | bytes 3145728 | tf_op jit(solution)/shard_map/psum | solution.py:15
  230.0 18.9 %collective-permute-start.5 = (bf16[2,64,512]{2,1,0:T(8,128)(2,1)S(1)}, bf16[2,64,512]{2,1,0:T(8,128)(2,1)S(1)}, u32[]{:S(2)}, u32[]{:S(2)}) collective-permute-start(bf16[2,64,512]{2,1,0:T(8,128)(2,1)S(1)} %copy-done.9), channel_id=1, source_target_pairs={{0,3},{1,4},{2,5},{3,6},{4,7},{5,8},{6,9},{7,10},{8,11},{9,12},{10... | collective-permute-start | bytes 393224 | tf_op jit(solution)/shard_map/ppermute | solution.py:20
  231.9 24.3 %collective-permute-start.8 = (bf16[2,64,512]{2,1,0:T(8,128)(2,1)S(1)}, bf16[2,64,512]{2,1,0:T(8,128)(2,1)S(1)}, u32[]{:S(2)}, u32[]{:S(2)}) collective-permute-start(bf16[2,64,512]{2,1,0:T(8,128)(2,1)S(1)} %copy-done.1), channel_id=1, source_target_pairs={{0,8},{1,9},{2,10},{3,11},{4,12},{5,13},{6,14},{7,15},{8,16},{9,17... | collective-permute-start | bytes 393224 | tf_op jit(solution)/shard_map/ppermute | solution.py:20
  233.9 30.6 %collective-permute-start.9 = (bf16[2,64,512]{2,1,0:T(8,128)(2,1)S(1)}, bf16[2,64,512]{2,1,0:T(8,128)(2,1)S(1)}, u32[]{:S(2)}, u32[]{:S(2)}) collective-permute-start(bf16[2,64,512]{2,1,0:T(8,128)(2,1)S(1)} %copy-done.1), channel_id=1, source_target_pairs={{0,7},{1,8},{2,9},{3,10},{4,11},{5,12},{6,13},{7,14},{8,15},{9,16}... | collective-permute-start | bytes 393224 | tf_op jit(solution)/shard_map/ppermute | solution.py:20
  235.9 34.7 %collective-permute-start.10 = (bf16[2,64,512]{2,1,0:T(8,128)(2,1)S(1)}, bf16[2,64,512]{2,1,0:T(8,128)(2,1)S(1)}, u32[]{:S(2)}, u32[]{:S(2)}) collective-permute-start(bf16[2,64,512]{2,1,0:T(8,128)(2,1)S(1)} %copy-done.1), channel_id=1, source_target_pairs={{0,6},{1,7},{2,8},{3,9},{4,10},{5,11},{6,12},{7,13},{8,14},{9,15},... | collective-permute-start | bytes 393224 | tf_op jit(solution)/shard_map/ppermute | solution.py:20
  239.3 36.8 %collective-permute-start.11 = (bf16[2,64,512]{2,1,0:T(8,128)(2,1)S(1)}, bf16[2,64,512]{2,1,0:T(8,128)(2,1)S(1)}, u32[]{:S(2)}, u32[]{:S(2)}) collective-permute-start(bf16[2,64,512]{2,1,0:T(8,128)(2,1)S(1)} %copy-done.1), channel_id=1, source_target_pairs={{0,5},{1,6},{2,7},{3,8},{4,9},{5,10},{6,11},{7,12},{8,13},{9,14},{... | collective-permute-start | bytes 393224 | tf_op jit(solution)/shard_map/ppermute | solution.py:20
  248.9 34.1 %copy-start.6 = (bf16[2,64,512]{2,1,0:T(8,128)(2,1)}, bf16[2,64,512]{2,1,0:T(8,128)(2,1)S(1)}, u32[]{:S(2)}) copy-start(bf16[2,64,512]{2,1,0:T(8,128)(2,1)S(1)} %collective-permute-done.5) | copy-start | bytes 393220
  248.9 29.7 %collective-permute-start.12 = (bf16[2,64,512]{2,1,0:T(8,128)(2,1)S(1)}, bf16[2,64,512]{2,1,0:T(8,128)(2,1)S(1)}, u32[]{:S(2)}, u32[]{:S(2)}) collective-permute-start(bf16[2,64,512]{2,1,0:T(8,128)(2,1)S(1)} %copy-done.1), channel_id=1, source_target_pairs={{0,4},{1,5},{2,6},{3,7},{4,8},{5,9},{6,10},{7,11},{8,12},{9,13},{1... | collective-permute-start | bytes 393224 | tf_op jit(solution)/shard_map/ppermute | solution.py:20
  256.2 25.4 %collective-permute-start.13 = (bf16[2,64,512]{2,1,0:T(8,128)(2,1)S(1)}, bf16[2,64,512]{2,1,0:T(8,128)(2,1)S(1)}, u32[]{:S(2)}, u32[]{:S(2)}) collective-permute-start(bf16[2,64,512]{2,1,0:T(8,128)(2,1)S(1)} %copy-done.1), channel_id=1, source_target_pairs={{0,3},{1,4},{2,5},{3,6},{4,7},{5,8},{6,9},{7,10},{8,11},{9,12},{10... | collective-permute-start | bytes 393224 | tf_op jit(solution)/shard_map/ppermute | solution.py:20
  264.6 561.4 %collective-permute-start.6 = (bf16[2,64,512]{2,1,0:T(8,128)(2,1)S(1)}, bf16[2,64,512]{2,1,0:T(8,128)(2,1)S(1)}, u32[]{:S(2)}, u32[]{:S(2)}) collective-permute-start(bf16[2,64,512]{2,1,0:T(8,128)(2,1)S(1)} %copy-done.9), channel_id=1, source_target_pairs={{0,2},{1,3},{2,4},{3,5},{4,6},{5,7},{6,8},{7,9},{8,10},{9,11},{10,... | collective-permute-start | bytes 393224 | tf_op jit(solution)/shard_map/ppermute | solution.py:20
  270.6 555.4 %collective-permute-start.14 = (bf16[2,64,512]{2,1,0:T(8,128)(2,1)S(1)}, bf16[2,64,512]{2,1,0:T(8,128)(2,1)S(1)}, u32[]{:S(2)}, u32[]{:S(2)}) collective-permute-start(bf16[2,64,512]{2,1,0:T(8,128)(2,1)S(1)} %copy-done.1), channel_id=1, source_target_pairs={{0,2},{1,3},{2,4},{3,5},{4,6},{5,7},{6,8},{7,9},{8,10},{9,11},{10,... | collective-permute-start | bytes 393224 | tf_op jit(solution)/shard_map/ppermute | solution.py:20
  276.1 549.9 %collective-permute-start.15 = (bf16[2,64,512]{2,1,0:T(8,128)(2,1)S(1)}, bf16[2,64,512]{2,1,0:T(8,128)(2,1)S(1)}, u32[]{:S(2)}, u32[]{:S(2)}) collective-permute-start(bf16[2,64,512]{2,1,0:T(8,128)(2,1)S(1)} %copy-done.1), channel_id=1, source_target_pairs={{0,1},{1,2},{2,3},{3,4},{4,5},{5,6},{6,7},{7,8},{8,9},{9,10},{10,1... | collective-permute-start | bytes 393224 | tf_op jit(solution)/shard_map/ppermute | solution.py:20
  278.6 547.4 %collective-permute-start.7 = (bf16[2,64,512]{2,1,0:T(8,128)(2,1)S(1)}, bf16[2,64,512]{2,1,0:T(8,128)(2,1)S(1)}, u32[]{:S(2)}, u32[]{:S(2)}) collective-permute-start(bf16[2,64,512]{2,1,0:T(8,128)(2,1)S(1)} %copy-done.9), channel_id=1, source_target_pairs={{0,1},{1,2},{2,3},{3,4},{4,5},{5,6},{6,7},{7,8},{8,9},{9,10},{10,1... | collective-permute-start | bytes 393224 | tf_op jit(solution)/shard_map/ppermute | solution.py:20
  281.6 2.9 copy-start.4
  283.1 3.2 copy-start.7
  283.1 3.2 slice-start.1
  285.3 1.0 copy-start.17
  824.4 0.9 copy-start.5
  824.4 0.9 slice-start
  826.0 3.5 copy-start.3
  826.0 3.5 copy-start.15
  829.5 2.9 copy-start.10
  831.3 0.8 copy-start
  1387.5 2.1 copy-start.14
  1387.5 2.1 copy-start.13
  1387.5 2.1 copy-start.12
  1388.6 1.1 copy-start.11
  1395.6 2.5 copy-start.20
  1402.8 10.1 copy-start.16
Sparse Core Ops, SparseCore 0:
  229.2 580.6 all-reduce.19
  824.5 562.9 all-reduce.21
